TPU v7x, 256 devices: a whole 4x4x8 slice. The times are simulated.
256 devices in a mesh: chrom: 4 (over x), snp: 64 (over z, y, core).
Axes of the slice: x: 4, y: 4, z: 8, core: 2. Of those that a mesh axis runs over, the one named last changes fastest.
Arguments:
- genotypes: bfloat16 [12288, 131072], P(None, ('chrom', 'snp')), may hold values from 0 to 2, as said below
- probes: bfloat16 [131072, 128], P(('chrom', 'snp')), may hold values from -4 to 4
Outputs:
- unit_basis: float32 [131072, 128], P(('chrom', 'snp'))
- range_log_norms: float32 [128], replicated
Inputs may be any that keep to these rules, and one draw needn't show every extreme that they name: `genotypes`: every entry is a dosage 0, 1 or 2.
All inputs are finite; a program needn't handle non-finite values.
Results may differ from a plain program's by a relative error of at most 0.0034.
The roundings to bfloat16 on the way count: a program that leaves them out, or rounds other values in their place, can miss the bound.
Values sent between devices are 32-bit elements; how exact they have to be, the bound alone decides.
No kernel may reach another device: no remote copies, remote signals or barrier semaphores. Data moves between devices by JAX's collectives and lax.ppermute only.
A program may use at most 128 MiB of HBM per device.

v0:
```python
import math
import jax
import jax.numpy as jnp
from jax import lax
from jax.sharding import PartitionSpec as P


def standardize(block):
    values = block.astype(jnp.float32)
    column_mean = jnp.mean(values, axis=0, keepdims=True)
    centered = values - column_mean
    spread = jnp.mean(centered * centered, axis=0, keepdims=True)
    return (centered * (spread + 1e-05) ** (-0.125)).astype(jnp.bfloat16)


def split_parts(sketch):
    sketch_high = lax.optimization_barrier(sketch.astype(jnp.bfloat16))
    remainder = sketch - sketch_high.astype(jnp.float32)
    sketch_mid = lax.optimization_barrier(remainder.astype(jnp.bfloat16))
    sketch_low = (remainder - sketch_mid.astype(jnp.float32)).astype(jnp.bfloat16)
    return jnp.concatenate([sketch_high, sketch_mid, sketch_low], axis=1)


def column_gram(matrix):
    return lax.dot_general(
        matrix,
        matrix,
        (((0,), (0,)), ((), ())),
        precision=lax.Precision.HIGHEST,
        preferred_element_type=jnp.float32,
    )


def unit_columns(matrix, gram_matrix):
    lower_factor = jnp.linalg.cholesky(gram_matrix)
    return lax.linalg.triangular_solve(
        lower_factor, matrix, left_side=False, lower=True, transpose_a=True
    )


def body(genotypes, probes):
    scaled = standardize(genotypes)
    width = probes.shape[1]
    partial_sketch = jnp.dot(scaled, probes, preferred_element_type=jnp.float32)
    sketch = lax.psum(partial_sketch, ("chrom", "snp"))
    sketch_parts = split_parts(sketch)
    product = lax.dot_general(
        scaled, sketch_parts, (((0,), (0,)), ((), ())), preferred_element_type=jnp.float32
    )
    range_rows = product[:, :width] + product[:, width : 2 * width] + product[:, 2 * width :]
    total_snps = range_rows.shape[0] * lax.axis_size("chrom") * lax.axis_size("snp")
    gram_first = lax.psum(column_gram(range_rows), ("chrom", "snp"))
    range_log_norms = 0.1 * jnp.log(jnp.diagonal(gram_first) / total_snps)
    first_basis = unit_columns(range_rows, gram_first)
    gram_second = lax.psum(column_gram(first_basis), ("chrom", "snp"))
    second_basis = unit_columns(first_basis, gram_second)
    return (second_basis * math.sqrt(total_snps), range_log_norms)


def solution(mesh):
    return jax.shard_map(
        body,
        mesh=mesh,
        in_specs=(P(None, ("chrom", "snp")), P(("chrom", "snp"), None)),
        out_specs=(P(("chrom", "snp"), None), P()),
        check_vma=False,
    )
```

profile of v0, /device:TPU:1, one launch (start us, length us, event | category | flops | bytes accessed | tf_op | source)
XLA Modules:
  0.0 860.5 jit_solution(15291087792489266892)
XLA Ops:
  7.2 0.0 copy-start
  7.2 0.0 all-reduce.4.cloned.1.call-start
  7.2 0.0 copy-start.2
  7.2 7.9 convert_reduce_fusion
  15.2 0.4 copy-done.2
  15.6 3.6 fusion.2
  19.2 0.0 copy-done
  19.2 5.3 fusion.6
  24.5 0.0 all-reduce.4.cloned.1.call-update
  24.5 0.0 all-reduce.6.cloned.1.call-start
  24.6 277.4 %all-reduce.4.cloned.1.call-done = f32[12288,128]{1,0:T(8,128)} async-done(((f32[12288,128]{1,0:T(8,128)}), f32[12288,128]{1,0:T(8,128)}) %all-reduce.4.cloned.1.call-update) | async-done | bytes 6291472 | tf_op jit(solution)/shard_map/psum | solution.py:45
  302.0 0.0 copy-start.1
  302.0 3.2 convert_element_type.23
  305.1 1.5 copy-done.1
  306.6 0.8 fusion.13
  307.5 1.3 subtract_convert_fusion
  308.7 11.3 %fusion.4 = f32[512,384]{1,0:T(8,128)S(1)} fusion(bf16[12288,512]{1,0:T(8,128)(2,1)} %param.5, f32[512]{0:T(512)S(1)} %add_power_fusion, f32[512]{0:T(512)S(1)} %broadcast_multiply_fusion, bf16[12288,128]{1,0:T(8,128)(2,1)S(1)} %subtract_convert_fusion, bf16[12288,128]{1,0:T(8,128)(2,1)S(1)} %fusion.13, bf16[12288,128]{1,0:T(8,128)(2,1)S(1)} %convert_element_type.23), kind=kOutput, calls=%fused_computation.7 | convolution fusion | flops 4885315584 | bytes 22810624 | tf_op jit(solution)/shard_map/dot_general | solution.py:47
  320.1 1.2 fusion.24
  321.3 0.0 all-reduce.6.cloned.1.call-update
  321.3 0.2 all-reduce.8.cloned.1.call-start
  321.6 242.2 %all-reduce.6.cloned.1.call-done = f32[128,128]{0,1:T(8,128)} async-done(((f32[128,128]{0,1:T(8,128)}), f32[128,128]{0,1:T(8,128)}) %all-reduce.6.cloned.1.call-update) | async-done | bytes 65552 | tf_op jit(solution)/shard_map/psum | solution.py:52
  563.8 0.9 copy.10
  564.8 0.9 fusion.20
  565.6 11.7 %cholesky.44 = f32[128,128]{1,0:T(8,128)S(1)} custom-call(f32[128,128]{1,0:T(8,128)S(1)} %fusion.20), custom_call_target="Cholesky" | custom-call | tf_op jit(solution)/shard_map/jit(cholesky)/cholesky | solution.py:35
  577.4 0.6 compare_reduce_fusion.1
  578.0 0.7 fusion.15
  578.7 9.8 %custom-call.8 = f32[1,128,128]{1,2,0:T(8,128)S(1)} custom-call(f32[1,128,128]{2,1,0:T(8,128)S(1)} %fusion.15), custom_call_target="InvertDiagBlocksLowerTriangular" | custom-call | tf_op jit(solution)/shard_map/triangular_solve/custom-call.0 | solution.py:36
  588.5 0.4 convolution_bitcast_fusion.1
  588.9 1.0 fusion.25
  589.9 0.0 all-reduce.8.cloned.1.call-update
  590.0 1.9 gather_fusion
  591.9 0.5 log_multiply_fusion
  592.4 235.7 %all-reduce.8.cloned.1.call-done = f32[128,128]{0,1:T(8,128)} async-done(((f32[128,128]{0,1:T(8,128)}), f32[128,128]{0,1:T(8,128)}) %all-reduce.8.cloned.1.call-update) | async-done | bytes 65552 | tf_op jit(solution)/shard_map/psum | solution.py:55
  828.1 0.9 copy.12
  829.0 0.9 fusion.18
  829.9 11.7 %cholesky.55 = f32[128,128]{1,0:T(8,128)S(1)} custom-call(f32[128,128]{1,0:T(8,128)S(1)} %fusion.18), custom_call_target="Cholesky" | custom-call | tf_op jit(solution)/shard_map/jit(cholesky)/cholesky | solution.py:35
  841.6 0.6 compare_reduce_fusion
  842.3 0.7 fusion.16
  842.9 9.8 %custom-call.9 = f32[1,128,128]{1,2,0:T(8,128)S(1)} custom-call(f32[1,128,128]{2,1,0:T(8,128)S(1)} %fusion.16), custom_call_target="InvertDiagBlocksLowerTriangular" | custom-call | tf_op jit(solution)/shard_map/triangular_solve/custom-call.0 | solution.py:36
  852.7 0.4 fusion.14
  853.2 0.8 copy.13
  (5 shorter events, 0.1 us)
Async XLA Ops:
  7.2 12.0 %copy-start = (bf16[512,128]{1,0:T(8,128)(2,1)S(1)}, bf16[512,128]{1,0:T(8,128)(2,1)}, u32[]{:S(2)}) copy-start(bf16[512,128]{1,0:T(8,128)(2,1)} %param.6) | copy-start | bytes 393220
  7.2 294.8 %all-reduce.4.cloned.1.call-start = ((), (), s32[]{:S(2)}) async-start(), calls=%async_computation | async-start | bytes 12582912 | tf_op jit(solution)/shard_map/psum | solution.py:45
  7.2 8.4 copy-start.2
  24.5 539.3 %all-reduce.6.cloned.1.call-start = ((), (), s32[]{:S(2)}) async-start(), calls=%async_computation.1 | async-start | bytes 131072 | tf_op jit(solution)/shard_map/psum | solution.py:52
  302.0 4.6 copy-start.1
  321.3 506.8 %all-reduce.8.cloned.1.call-start = ((), (), s32[]{:S(2)}) async-start(), calls=%async_computation.2 | async-start | bytes 131072 | tf_op jit(solution)/shard_map/psum | solution.py:55
Sparse Core Ops, SparseCore 0:
  24.6 277.2 all-reduce.3
  321.5 242.3 all-reduce.5
  590.1 237.9 all-reduce.7
where the time goes:
time: 861 us
  waiting for transfers between devices  755 us (88%)
  other arithmetic  64.7 us (8%)
  matrix products  19.7 us (2%)
  between operations  13.9 us (2%)
    psum x1, waiting for transfers between devices, body(): sketch = lax.psum(partial_sketch, ('chrom', 'snp'))  277 us
    psum x1, waiting for transfers between devices, body(): gram_first = lax.psum(column_gram(range_rows), ('chrom', 'snp'))  242 us
    psum x1, waiting for transfers between devices, body(): gram_second = lax.psum(column_gram(first_basis), ('chrom', 'snp'))  236 us
    another operation x6, other arithmetic, unit_columns(): lower_factor = jnp.linalg.cholesky(gram_matrix)  24.8 us
    another operation x4, other arithmetic, unit_columns(): lax.linalg.triangular_solve(lower_factor, matrix, left_side=False, lower=...  20.9 us
  transfers between devices with their start and end apart: 3, of which 3 were waited for; matrix products, arithmetic and copies ran while one was open for 0% of the time, Pallas kernels for 0%

commit v1 on v0

--- a/solution.py
+++ b/solution.py
@@ -49,7 +49,7 @@
     )
     range_rows = product[:, :width] + product[:, width : 2 * width] + product[:, 2 * width :]
     total_snps = range_rows.shape[0] * lax.axis_size("chrom") * lax.axis_size("snp")
-    gram_first = lax.psum(column_gram(range_rows), ("chrom", "snp"))
+    gram_first = lax.psum(lax.psum(column_gram(range_rows), "snp"), "chrom")
     range_log_norms = 0.1 * jnp.log(jnp.diagonal(gram_first) / total_snps)
     first_basis = unit_columns(range_rows, gram_first)
     gram_second = lax.psum(column_gram(first_basis), ("chrom", "snp"))

time: 861 us -> 840 us (0.976)
  waiting for transfers between devices: 755 us -> 734 us
    psum x1 -> x2, waiting for transfers between devices: 242 us -> 215 us  [body(): gram_first = lax.psum(lax.psum(column_gram(range_rows), 'snp'), 'chrom')]
  transfers between devices with their start and end apart: 3 -> 4, of which waited for: 3 -> 4; matrix products, arithmetic and copies ran while one was open for 0% -> 0% of each run, Pallas kernels for 0% -> 0%
where the time goes in v1:
time: 840 us; the launch traced here: 839 us
  waiting for transfers between devices  734 us (87%)
  other arithmetic  64.7 us (8%)
  matrix products  19.7 us (2%)
  between operations  13.9 us (2%)
    psum x1, waiting for transfers between devices, body(): sketch = lax.psum(partial_sketch, ('chrom', 'snp'))  277 us
    psum x1, waiting for transfers between devices, body(): gram_second = lax.psum(column_gram(first_basis), ('chrom', 'snp'))  242 us
    psum x2, waiting for transfers between devices, body(): gram_first = lax.psum(lax.psum(column_gram(range_rows), 'snp'), 'chrom')  215 us
    another operation x6, other arithmetic, unit_columns(): lower_factor = jnp.linalg.cholesky(gram_matrix)  24.8 us
    another operation x4, other arithmetic, unit_columns(): lax.linalg.triangular_solve(lower_factor, matrix, left_side=False, lower=...  20.9 us
  transfers between devices with their start and end apart: 4, of which 4 were waited for; matrix products, arithmetic and copies ran while one was open for 0% of the time, Pallas kernels for 0%

profile of v1, /device:TPU:1, one launch (start us, length us, event | category | flops | bytes accessed | tf_op | source)
XLA Modules:
  0.0 839.2 jit_solution(18298855735481685165)
XLA Ops:
  7.2 0.0 copy-start
  7.2 0.0 all-reduce.5.cloned.1.call-start
  7.2 0.0 copy-start.2
  7.2 7.9 convert_reduce_fusion
  15.2 0.4 copy-done.2
  15.6 3.6 fusion.2
  19.2 0.0 copy-done
  19.2 5.3 fusion.6
  24.5 0.0 all-reduce.5.cloned.1.call-update
  24.5 0.0 all-reduce.7.cloned.1.call-start
  24.6 277.4 %all-reduce.5.cloned.1.call-done = f32[12288,128]{1,0:T(8,128)} async-done(((f32[12288,128]{1,0:T(8,128)}), f32[12288,128]{1,0:T(8,128)}) %all-reduce.5.cloned.1.call-update) | async-done | bytes 6291472 | tf_op jit(solution)/shard_map/psum | solution.py:45
  302.0 0.0 copy-start.1
  302.0 3.2 convert_element_type.23
  305.1 1.5 copy-done.1
  306.6 0.8 fusion.13
  307.5 1.3 subtract_convert_fusion
  308.7 11.3 %fusion.4 = f32[512,384]{1,0:T(8,128)S(1)} fusion(bf16[12288,512]{1,0:T(8,128)(2,1)} %param.5, f32[512]{0:T(512)S(1)} %add_power_fusion, f32[512]{0:T(512)S(1)} %broadcast_multiply_fusion, bf16[12288,128]{1,0:T(8,128)(2,1)S(1)} %subtract_convert_fusion, bf16[12288,128]{1,0:T(8,128)(2,1)S(1)} %fusion.13, bf16[12288,128]{1,0:T(8,128)(2,1)S(1)} %convert_element_type.23), kind=kOutput, calls=%fused_computation.7 | convolution fusion | flops 4885315584 | bytes 22810624 | tf_op jit(solution)/shard_map/dot_general | solution.py:47
  320.1 1.2 fusion.24
  321.3 0.0 all-reduce.7.cloned.1.call-update
  321.3 0.0 all-reduce.9.cloned.1.call-start
  321.4 171.7 %all-reduce.7.cloned.1.call-done = f32[128,128]{0,1:T(8,128)} async-done(((f32[128,128]{0,1:T(8,128)}), f32[128,128]{0,1:T(8,128)}) %all-reduce.7.cloned.1.call-update) | async-done | bytes 65552 | tf_op jit(solution)/shard_map/psum | solution.py:52
  493.1 0.0 all-reduce.9.cloned.1.call-update
  493.1 0.2 all-reduce.11.cloned.1.call-start
  493.3 43.0 %all-reduce.9.cloned.1.call-done = f32[128,128]{0,1:T(8,128)} async-done(((f32[128,128]{0,1:T(8,128)}), f32[128,128]{0,1:T(8,128)}) %all-reduce.9.cloned.1.call-update) | async-done | bytes 65552 | tf_op jit(solution)/shard_map/psum | solution.py:52
  536.3 0.9 copy.10
  537.3 0.9 fusion.20
  538.1 11.7 %cholesky.44 = f32[128,128]{1,0:T(8,128)S(1)} custom-call(f32[128,128]{1,0:T(8,128)S(1)} %fusion.20), custom_call_target="Cholesky" | custom-call | tf_op jit(solution)/shard_map/jit(cholesky)/cholesky | solution.py:35
  549.9 0.6 compare_reduce_fusion.1
  550.5 0.7 fusion.15
  551.2 9.8 %custom-call.8 = f32[1,128,128]{1,2,0:T(8,128)S(1)} custom-call(f32[1,128,128]{2,1,0:T(8,128)S(1)} %fusion.15), custom_call_target="InvertDiagBlocksLowerTriangular" | custom-call | tf_op jit(solution)/shard_map/triangular_solve/custom-call.0 | solution.py:36
  561.0 0.4 convolution_bitcast_fusion.1
  561.4 1.0 fusion.25
  562.4 0.0 all-reduce.11.cloned.1.call-update
  562.5 1.9 gather_fusion
  564.4 0.5 log_multiply_fusion
  564.9 241.8 %all-reduce.11.cloned.1.call-done = f32[128,128]{0,1:T(8,128)} async-done(((f32[128,128]{0,1:T(8,128)}), f32[128,128]{0,1:T(8,128)}) %all-reduce.11.cloned.1.call-update) | async-done | bytes 65552 | tf_op jit(solution)/shard_map/psum | solution.py:55
  806.8 0.9 copy.12
  807.7 0.9 fusion.18
  808.5 11.7 %cholesky.55 = f32[128,128]{1,0:T(8,128)S(1)} custom-call(f32[128,128]{1,0:T(8,128)S(1)} %fusion.18), custom_call_target="Cholesky" | custom-call | tf_op jit(solution)/shard_map/jit(cholesky)/cholesky | solution.py:35
  820.3 0.6 compare_reduce_fusion
  820.9 0.7 fusion.16
  821.6 9.8 %custom-call.9 = f32[1,128,128]{1,2,0:T(8,128)S(1)} custom-call(f32[1,128,128]{2,1,0:T(8,128)S(1)} %fusion.16), custom_call_target="InvertDiagBlocksLowerTriangular" | custom-call | tf_op jit(solution)/shard_map/triangular_solve/custom-call.0 | solution.py:36
  831.4 0.4 fusion.14
  831.8 0.8 copy.13
  (5 shorter events, 0.1 us)
Async XLA Ops:
  7.2 12.0 %copy-start = (bf16[512,128]{1,0:T(8,128)(2,1)S(1)}, bf16[512,128]{1,0:T(8,128)(2,1)}, u32[]{:S(2)}) copy-start(bf16[512,128]{1,0:T(8,128)(2,1)} %param.6) | copy-start | bytes 393220
  7.2 294.8 %all-reduce.5.cloned.1.call-start = ((), (), s32[]{:S(2)}) async-start(), calls=%async_computation | async-start | bytes 12582912 | tf_op jit(solution)/shard_map/psum | solution.py:45
  7.2 8.4 copy-start.2
  24.5 468.6 %all-reduce.7.cloned.1.call-start = ((), (), s32[]{:S(2)}) async-start(), calls=%async_computation.1 | async-start | bytes 131072 | tf_op jit(solution)/shard_map/psum | solution.py:52
  302.0 4.6 copy-start.1
  321.3 215.0 %all-reduce.9.cloned.1.call-start = ((), (), s32[]{:S(2)}) async-start(), calls=%async_computation.2 | async-start | bytes 131072 | tf_op jit(solution)/shard_map/psum | solution.py:52
  493.1 313.7 %all-reduce.11.cloned.1.call-start = ((), (), s32[]{:S(2)}) async-start(), calls=%async_computation.3 | async-start | bytes 131072 | tf_op jit(solution)/shard_map/psum | solution.py:55
Sparse Core Ops, SparseCore 0:
  24.6 277.2 all-reduce.4
  321.5 171.5 all-reduce.6
  495.4 40.8 all-reduce.8
  562.6 244.1 all-reduce.10
